TPU v7x, 32 devices: a whole 2x2x4 slice. The times are simulated.
32 devices in a mesh: tm: 8 (over z, x), space: 4 (over y, core).
Axes of the slice: x: 2, y: 2, z: 4, core: 2. Of those that a mesh axis runs over, the one named last changes fastest.
Arguments:
- snapshots: float32 [4224, 4096], P('tm', 'space')
- starts: int32 [32], replicated, may hold values from 0 to 3968, as said below
- freq_lines: int32 [128], replicated, may hold values from 0 to 128, as said below
Outputs:
- power_density: float32 [128, 4096], P(None, ('space', 'tm'))
- gram_matrices: float32 [2, 128, 32, 32], P(None, 'tm')
Inputs may be any that keep to these rules, and one draw needn't show every extreme that they name: starts never fall, and block b starts at most 64 snapshots away from b * 128; the first block starts at 0 and the last at 3968. `freq_lines`: distinct line numbers in any order; 0 and 128 are among them.
All inputs are finite; a program needn't handle non-finite values.
Results may differ from a plain program's by a relative error of at most 0.0001.
Values sent between devices are 32-bit elements; how exact they have to be, the bound alone decides.
No kernel may reach another device: no remote copies, remote signals or barrier semaphores. Data moves between devices by JAX's collectives and lax.ppermute only.
A program may use at most 64 MiB of HBM per device.

v0:
```python
import math
import jax
import jax.numpy as jnp
from jax import lax
from jax.sharding import PartitionSpec as P

NFFT = 256
NF = 128
NB = 32


def spectral_table(freq_lines):
    moments = jnp.arange(NFFT, dtype=jnp.int32)
    cycle = freq_lines[:, None] * moments[None, :] % NFFT
    angles = 2.0 * math.pi / NFFT * cycle.astype(jnp.float32)
    window = 0.5 - 0.5 * jnp.cos(2.0 * math.pi / NFFT * moments.astype(jnp.float32))
    window = window / jnp.sqrt(jnp.sum(window * window))
    return jnp.concatenate(
        [window[None, :] * jnp.cos(angles), -window[None, :] * jnp.sin(angles)], axis=0
    )


def block_spectra(series, starts, table):
    offsets = starts[:, None] + jnp.arange(NFFT, dtype=jnp.int32)[None, :]
    blocks = series[offsets]
    return jnp.einsum("kt,btp->kbp", table, blocks, precision=lax.Precision.HIGHEST)


def local_terms(spectra, factor):
    highest = lax.Precision.HIGHEST
    real_part = spectra[:NF]
    imag_part = spectra[NF:]
    power = jnp.sum(real_part * real_part + imag_part * imag_part, axis=1) / NB
    gram_real = jnp.einsum("fbp,fcp->fbc", real_part, real_part, precision=highest) + jnp.einsum(
        "fbp,fcp->fbc", imag_part, imag_part, precision=highest
    )
    gram_imag = jnp.einsum("fbp,fcp->fbc", real_part, imag_part, precision=highest) - jnp.einsum(
        "fbp,fcp->fbc", imag_part, real_part, precision=highest
    )
    return (power, jnp.stack([gram_real, gram_imag]) * factor)


def body(snapshots, starts, freq_lines):
    groups = lax.axis_size("tm")
    columns = snapshots.shape[1] // groups
    table = spectral_table(freq_lines)
    arranged = snapshots.reshape(snapshots.shape[0], groups, columns)
    spectra = block_spectra(
        lax.all_to_all(arranged, "tm", split_axis=1, concat_axis=0, tiled=True)[:, 0, :],
        starts,
        table,
    )
    total_points = columns * groups * lax.axis_size("space")
    power_density, own_gram = local_terms(spectra, 1.0 / (NB * total_points))
    per_device = NF // groups
    summed = lax.psum(own_gram, ("tm", "space"))
    gram_matrices = lax.dynamic_slice_in_dim(
        summed, lax.axis_index("tm") * per_device, per_device, 1
    )
    return (power_density, gram_matrices)


def solution(mesh):
    placed = (P("tm", "space"), P(), P())
    return jax.shard_map(
        body,
        mesh=mesh,
        in_specs=placed,
        out_specs=(P(None, ("space", "tm")), P(None, "tm", None, None)),
        check_vma=False,
    )
```

profile of v0, /device:TPU:0, one launch (start us, length us, event | category | flops | bytes accessed | tf_op | source)
XLA Modules:
  0.0 276.6 jit_solution(2760193698736418181)
XLA Ops:
  7.2 0.0 copy-start
  7.2 1.6 copy-done
  8.8 1.5 copy_bitcast_fusion
  10.3 7.4 %all-to-all-start = ((f32[528,8,128]{2,0,1:T(8,128)}), f32[528,8,128]{2,0,1:T(8,128)}, u32[]{:S(2)}, u32[]{:S(2)}) async-start(f32[528,8,128]{2,0,1:T(8,128)} %copy_bitcast_fusion), calls=%async_computation | async-start | bytes 4325376 | tf_op jit(solution)/shard_map/all_to_all | solution.py:49
  17.7 0.0 all-reduce.2.cloned.1.call-start
  17.7 0.6 multiply_reduce_fusion
  19.1 0.1 fusion.25
  19.2 0.6 cosine_multiply_fusion
  19.9 47.6 %all-to-all-done = f32[528,8,128]{2,0,1:T(8,128)} async-done(((f32[528,8,128]{2,0,1:T(8,128)}), f32[528,8,128]{2,0,1:T(8,128)}, u32[]{:S(2)}, u32[]{:S(2)}) %all-to-all-start) | async-done | bytes 2162720 | tf_op jit(solution)/shard_map/all_to_all | solution.py:49
  67.4 29.4 %gather_fusion = f32[8192,128]{1,0:T(8,128)} fusion(f32[4224,128]{1,0:T(8,128)} %bitcast.3, s32[8192]{0:T(1024)S(1)} %broadcast_clamp_fusion), kind=kCustom, calls=%fused_computation | custom fusion | bytes 8421376 | tf_op jit(solution)/shard_map/gather | solution.py:25
  96.8 5.6 %fusion.16 = f32[256,32,128]{2,0,1:T(8,128)S(1)} fusion(f32[32,256,128]{2,1,0:T(8,128)} %bitcast.23, f32[128,256]{1,0:T(8,128)S(1)} %get-tuple-element.8, f32[128,256]{1,0:T(8,128)S(1)} %get-tuple-element.7), kind=kOutput, calls=%fused_computation.17 | convolution fusion | flops 3221291008 | bytes 8650752 | tf_op jit(solution)/shard_map/kt,btp->kbp/dot_general | solution.py:26
  102.4 0.7 fusion.29
  103.1 5.7 %fusion.4 = f32[128,32,32]{2,1,0:T(8,128)} fusion(f32[128,32,128]{2,0,1:T(8,128)S(1)} %get-tuple-element.6), kind=kOutput, calls=%fused_computation.9 | convolution fusion | flops 201326592 | bytes 2621440 | tf_op jit(solution)/shard_map/fbp,fcp->fbc/dot_general | solution.py:34
  108.8 5.7 %fusion = f32[128,32,32]{2,1,0:T(8,128)S(1)} fusion(f32[128,32,128]{2,0,1:T(8,128)S(1)} %get-tuple-element.6, f32[128,32,128]{2,0,1:T(8,128)S(1)} %get-tuple-element.4), kind=kOutput, calls=%fused_computation.5 | convolution fusion | flops 201326592 | bytes 4718592 | tf_op jit(solution)/shard_map/fbp,fcp->fbc/dot_general | solution.py:37
  114.5 7.2 %subtract_bitcast_fusion = f32[1,128,32,32]{3,2,1,0:T(8,128)} fusion(f32[128,32,32]{2,1,0:T(8,128)S(1)} %fusion, f32[128,32,128]{2,0,1:T(8,128)S(1)} %get-tuple-element.6, f32[128,32,128]{2,0,1:T(8,128)S(1)} %get-tuple-element.4), kind=kOutput, calls=%fused_computation.2 | convolution fusion | flops 201457664 | bytes 5242880 | tf_op jit(solution)/shard_map/fbp,fcp->fbc/dot_general | solution.py:37
  121.7 2.7 copy.33
  124.3 9.7 %add_bitcast_fusion = f32[1,128,32,32]{3,2,1,0:T(8,128)} fusion(f32[128,32,32]{2,1,0:T(8,128)} %fusion.4, f32[128,32,128]{2,0,1:T(8,128)} %copy-done.1), kind=kOutput, calls=%fused_computation.3 | convolution fusion | flops 201457664 | bytes 3145728 | tf_op jit(solution)/shard_map/fbp,fcp->fbc/dot_general | solution.py:34
  134.1 2.7 copy.32
  136.7 1.1 maximum_multiply_fusion
  137.8 0.0 all-reduce.2.cloned.1.call-update
  137.9 0.6 broadcast_multiply_fusion
  138.5 128.4 %all-reduce.2.cloned.1.call-done = f32[2,128,32,32]{1,3,2,0:T(8,128)} async-done(((f32[2,128,32,32]{1,3,2,0:T(8,128)}), f32[2,128,32,32]{1,3,2,0:T(8,128)}) %all-reduce.2.cloned.1.call-update) | async-done | bytes 1048592 | tf_op jit(solution)/shard_map/psum | solution.py:56
  266.9 1.6 constant_dynamic-slice_fusion
  268.5 1.2 copy.34
  (9 shorter events, 0.1 us)
Async XLA Ops:
  7.2 1.6 copy-start
  10.3 8.8 %copy-start.2 = (s32[32]{0:T(128)S(1)}, s32[32]{0:T(128)}, u32[]{:S(2)}) copy-start(s32[32]{0:T(128)} %param.4) | copy-start | bytes 388
  10.3 9.0 %copy-start.3 = (s32[128]{0:T(128)S(1)}, s32[128]{0:T(128)}, u32[]{:S(2)}) copy-start(s32[128]{0:T(128)} %param.5) | copy-start | bytes 1540
  10.3 57.1 %all-to-all-start = ((f32[528,8,128]{2,0,1:T(8,128)}), f32[528,8,128]{2,0,1:T(8,128)}, u32[]{:S(2)}, u32[]{:S(2)}) async-start(f32[528,8,128]{2,0,1:T(8,128)} %copy_bitcast_fusion), calls=%async_computation | async-start | bytes 4325376 | tf_op jit(solution)/shard_map/all_to_all | solution.py:49
  17.7 249.3 %all-reduce.2.cloned.1.call-start = ((), (), s32[]{:S(2)}) async-start(), calls=%async_computation.1 | async-start | bytes 2097152 | tf_op jit(solution)/shard_map/psum | solution.py:56
  103.1 11.4 %copy-start.1 = (f32[128,32,128]{2,0,1:T(8,128)}, f32[128,32,128]{2,0,1:T(8,128)S(1)}, u32[]{:S(2)}) copy-start(f32[128,32,128]{2,0,1:T(8,128)S(1)} %get-tuple-element.4) | copy-start | bytes 6291460
Sparse Core Ops, SparseCore 0:
  138.0 128.9 all-reduce.1
where the time goes:
time: 277 us
  waiting for transfers between devices  176 us (64%)
  local copies, waits for them, and re-layouts  40.6 us (15%)
  matrix products  33.9 us (12%)
  between operations  14.8 us (5%)
  starting transfers between devices  7.42 us (3%)
  other arithmetic  3.87 us (1%)
    psum x1, waiting for transfers between devices, body(): summed = lax.psum(own_gram, ('tm', 'space'))  128 us
    all_to_all x1, waiting for transfers between devices, body(): lax.all_to_all(arranged, 'tm', split_axis=1, concat_axis=0, tiled=True)  47.6 us
    gather x1, local copies, waits for them, and re-layouts, block_spectra(): blocks = series[offsets]  29.4 us
    dot_general x1, matrix products, local_terms(): jnp.einsum('fbp,fcp->fbc', real_part, real_part, precision=highest)  9.72 us
    all_to_all x1, starting transfers between devices, body(): lax.all_to_all(arranged, 'tm', split_axis=1, concat_axis=0, tiled=True)  7.38 us
    dot_general x1, matrix products, local_terms(): jnp.einsum('fbp,fcp->fbc', real_part, imag_part, precision=highest)  7.21 us
    dot_general x1, matrix products, local_terms(): jnp.einsum('fbp,fcp->fbc', imag_part, imag_part, precision=highest)  5.68 us
    dot_general x1, matrix products, local_terms(): jnp.einsum('fbp,fcp->fbc', imag_part, real_part, precision=highest)  5.67 us
  transfers between devices with their start and end apart: 2, of which 2 were waited for; matrix products, arithmetic and copies ran while one was open for 1% of the time, Pallas kernels for 0%

commit v1 on v0

--- a/solution.py
+++ b/solution.py
@@ -53,7 +53,7 @@
     total_points = columns * groups * lax.axis_size("space")
     power_density, own_gram = local_terms(spectra, 1.0 / (NB * total_points))
     per_device = NF // groups
-    summed = lax.psum(own_gram, ("tm", "space"))
+    summed = lax.psum(lax.psum(own_gram, "space"), "tm")
     gram_matrices = lax.dynamic_slice_in_dim(
         summed, lax.axis_index("tm") * per_device, per_device, 1
     )

time: 277 us -> 265 us (0.957)
  waiting for transfers between devices: 176 us -> 165 us
    psum x1 -> x2, waiting for transfers between devices: 128 us -> 117 us  [body(): summed = lax.psum(lax.psum(own_gram, 'space'), 'tm')]
  transfers between devices with their start and end apart: 2 -> 3, of which waited for: 2 -> 3; matrix products, arithmetic and copies ran while one was open for 1% -> 1% of each run, Pallas kernels for 0% -> 0%
where the time goes in v1:
time: 265 us
  waiting for transfers between devices  165 us (62%)
  local copies, waits for them, and re-layouts  40.6 us (15%)
  matrix products  33.9 us (13%)
  between operations  14.8 us (6%)
  starting transfers between devices  7.46 us (3%)
  other arithmetic  3.87 us (1%)
    psum x2, waiting for transfers between devices, body(): summed = lax.psum(lax.psum(own_gram, 'space'), 'tm')  117 us
    all_to_all x1, waiting for transfers between devices, body(): lax.all_to_all(arranged, 'tm', split_axis=1, concat_axis=0, tiled=True)  47.6 us
    gather x1, local copies, waits for them, and re-layouts, block_spectra(): blocks = series[offsets]  29.4 us
    dot_general x1, matrix products, local_terms(): jnp.einsum('fbp,fcp->fbc', real_part, real_part, precision=highest)  9.72 us
    all_to_all x1, starting transfers between devices, body(): lax.all_to_all(arranged, 'tm', split_axis=1, concat_axis=0, tiled=True)  7.38 us
    dot_general x1, matrix products, local_terms(): jnp.einsum('fbp,fcp->fbc', real_part, imag_part, precision=highest)  7.21 us
    dot_general x1, matrix products, local_terms(): jnp.einsum('fbp,fcp->fbc', imag_part, imag_part, precision=highest)  5.68 us
    dot_general x1, matrix products, local_terms(): jnp.einsum('fbp,fcp->fbc', imag_part, real_part, precision=highest)  5.67 us
  transfers between devices with their start and end apart: 3, of which 3 were waited for; matrix products, arithmetic and copies ran while one was open for 1% of the time, Pallas kernels for 0%

profile of v1, /device:TPU:0, one launch (start us, length us, event | category | flops | bytes accessed | tf_op | source)
XLA Modules:
  0.0 265.1 jit_solution(7697171505018055000)
XLA Ops:
  7.2 1.6 copy-done
  8.8 1.5 copy_bitcast_fusion
  10.3 7.4 %all-to-all-start = ((f32[528,8,128]{2,0,1:T(8,128)}), f32[528,8,128]{2,0,1:T(8,128)}, u32[]{:S(2)}, u32[]{:S(2)}) async-start(f32[528,8,128]{2,0,1:T(8,128)} %copy_bitcast_fusion), calls=%async_computation | async-start | bytes 4325376 | tf_op jit(solution)/shard_map/all_to_all | solution.py:49
  17.7 0.0 all-reduce.3.cloned.1.call-start
  17.7 0.6 multiply_reduce_fusion
  19.1 0.1 fusion.25
  19.2 0.6 cosine_multiply_fusion
  19.9 47.6 %all-to-all-done = f32[528,8,128]{2,0,1:T(8,128)} async-done(((f32[528,8,128]{2,0,1:T(8,128)}), f32[528,8,128]{2,0,1:T(8,128)}, u32[]{:S(2)}, u32[]{:S(2)}) %all-to-all-start) | async-done | bytes 2162720 | tf_op jit(solution)/shard_map/all_to_all | solution.py:49
  67.4 29.4 %gather_fusion = f32[8192,128]{1,0:T(8,128)} fusion(f32[4224,128]{1,0:T(8,128)} %bitcast.3, s32[8192]{0:T(1024)S(1)} %broadcast_clamp_fusion), kind=kCustom, calls=%fused_computation | custom fusion | bytes 8421376 | tf_op jit(solution)/shard_map/gather | solution.py:25
  96.8 5.6 %fusion.16 = f32[256,32,128]{2,0,1:T(8,128)S(1)} fusion(f32[32,256,128]{2,1,0:T(8,128)} %bitcast.23, f32[128,256]{1,0:T(8,128)S(1)} %get-tuple-element.8, f32[128,256]{1,0:T(8,128)S(1)} %get-tuple-element.7), kind=kOutput, calls=%fused_computation.17 | convolution fusion | flops 3221291008 | bytes 8650752 | tf_op jit(solution)/shard_map/kt,btp->kbp/dot_general | solution.py:26
  102.4 0.7 fusion.29
  103.1 5.7 %fusion.4 = f32[128,32,32]{2,1,0:T(8,128)} fusion(f32[128,32,128]{2,0,1:T(8,128)S(1)} %get-tuple-element.6), kind=kOutput, calls=%fused_computation.9 | convolution fusion | flops 201326592 | bytes 2621440 | tf_op jit(solution)/shard_map/fbp,fcp->fbc/dot_general | solution.py:34
  108.8 5.7 %fusion = f32[128,32,32]{2,1,0:T(8,128)S(1)} fusion(f32[128,32,128]{2,0,1:T(8,128)S(1)} %get-tuple-element.6, f32[128,32,128]{2,0,1:T(8,128)S(1)} %get-tuple-element.4), kind=kOutput, calls=%fused_computation.5 | convolution fusion | flops 201326592 | bytes 4718592 | tf_op jit(solution)/shard_map/fbp,fcp->fbc/dot_general | solution.py:37
  114.5 7.2 %subtract_bitcast_fusion = f32[1,128,32,32]{3,2,1,0:T(8,128)} fusion(f32[128,32,32]{2,1,0:T(8,128)S(1)} %fusion, f32[128,32,128]{2,0,1:T(8,128)S(1)} %get-tuple-element.6, f32[128,32,128]{2,0,1:T(8,128)S(1)} %get-tuple-element.4), kind=kOutput, calls=%fused_computation.2 | convolution fusion | flops 201457664 | bytes 5242880 | tf_op jit(solution)/shard_map/fbp,fcp->fbc/dot_general | solution.py:37
  121.7 2.7 %copy.33 = f32[1,128,32,32]{1,3,2,0:T(8,128)S(1)} copy(f32[1,128,32,32]{3,2,1,0:T(8,128)} %subtract_bitcast_fusion) | data formatting | bytes 1048576 | tf_op jit(solution)/shard_map/stack | solution.py:40
  124.3 9.7 %add_bitcast_fusion = f32[1,128,32,32]{3,2,1,0:T(8,128)} fusion(f32[128,32,32]{2,1,0:T(8,128)} %fusion.4, f32[128,32,128]{2,0,1:T(8,128)} %copy-done.1), kind=kOutput, calls=%fused_computation.3 | convolution fusion | flops 201457664 | bytes 3145728 | tf_op jit(solution)/shard_map/fbp,fcp->fbc/dot_general | solution.py:34
  134.1 2.7 %copy.32 = f32[1,128,32,32]{1,3,2,0:T(8,128)S(1)} copy(f32[1,128,32,32]{3,2,1,0:T(8,128)} %add_bitcast_fusion) | data formatting | bytes 1048576 | tf_op jit(solution)/shard_map/stack | solution.py:40
  136.7 1.1 maximum_multiply_fusion
  137.9 0.0 all-reduce.5.cloned.1.call-start
  137.9 35.3 %all-reduce.3.cloned.1.call-done = f32[2,128,32,32]{1,3,2,0:T(8,128)} async-done(((f32[2,128,32,32]{1,3,2,0:T(8,128)}), f32[2,128,32,32]{1,3,2,0:T(8,128)}) %all-reduce.3.cloned.1.call-update) | async-done | bytes 1048592 | tf_op jit(solution)/shard_map/psum | solution.py:56
  173.2 0.6 broadcast_multiply_fusion
  173.9 81.7 %all-reduce.5.cloned.1.call-done = f32[2,128,32,32]{1,3,2,0:T(8,128)} async-done(((f32[2,128,32,32]{1,3,2,0:T(8,128)}), f32[2,128,32,32]{1,3,2,0:T(8,128)}) %all-reduce.5.cloned.1.call-update) | async-done | bytes 1048592 | tf_op jit(solution)/shard_map/psum | solution.py:56
  255.5 1.6 constant_dynamic-slice_fusion
  257.1 1.2 copy.34
  (12 shorter events, 0.1 us)
Async XLA Ops:
  7.2 1.6 copy-start
  10.3 8.8 %copy-start.2 = (s32[32]{0:T(128)S(1)}, s32[32]{0:T(128)}, u32[]{:S(2)}) copy-start(s32[32]{0:T(128)} %param.4) | copy-start | bytes 388
  10.3 9.0 %copy-start.3 = (s32[128]{0:T(128)S(1)}, s32[128]{0:T(128)}, u32[]{:S(2)}) copy-start(s32[128]{0:T(128)} %param.5) | copy-start | bytes 1540
  10.3 57.1 %all-to-all-start = ((f32[528,8,128]{2,0,1:T(8,128)}), f32[528,8,128]{2,0,1:T(8,128)}, u32[]{:S(2)}, u32[]{:S(2)}) async-start(f32[528,8,128]{2,0,1:T(8,128)} %copy_bitcast_fusion), calls=%async_computation | async-start | bytes 4325376 | tf_op jit(solution)/shard_map/all_to_all | solution.py:49
  17.7 155.5 %all-reduce.3.cloned.1.call-start = ((), (), s32[]{:S(2)}) async-start(), calls=%async_computation.1 | async-start | bytes 2097152 | tf_op jit(solution)/shard_map/psum | solution.py:56
  103.1 11.4 %copy-start.1 = (f32[128,32,128]{2,0,1:T(8,128)}, f32[128,32,128]{2,0,1:T(8,128)S(1)}, u32[]{:S(2)}) copy-start(f32[128,32,128]{2,0,1:T(8,128)S(1)} %get-tuple-element.4) | copy-start | bytes 6291460
  137.9 117.7 %all-reduce.5.cloned.1.call-start = ((), (), s32[]{:S(2)}) async-start(), calls=%async_computation.2 | async-start | bytes 2097152 | tf_op jit(solution)/shard_map/psum | solution.py:56
Sparse Core Ops, SparseCore 0:
  138.0 35.1 all-reduce.2
  177.1 78.3 all-reduce.4
